TPU v7x, 32 devices: a whole 2x2x4 slice. The times are simulated.
32 devices in a mesh: cond: 4 (over z), ty: 2 (over y), tx: 4 (over x, core).
Axes of the slice: x: 2, y: 2, z: 4, core: 2. Of those that a mesh axis runs over, the one named last changes fastest.
Arguments:
- mask_logits: float32 [1024, 2048], P('ty', 'tx'), may hold values from -8 to 8
- target_layout: int32 [1024, 2048], P('ty', 'tx'), may hold values 0 or 1
- density_weights: int32 [1024, 2048], P('ty', 'tx'), may hold values from 0 to 3, as said below
- socs_kernels: float32 [4, 12, 2, 24, 24], P('cond'), may hold values from -3 to 3
Outputs:
- logits_new: float32 [1024, 2048], P('ty', 'tx')
- mask_next: bfloat16 [1024, 2048], P('ty', 'tx')
Inputs may be any that keep to these rules, and one draw needn't show every extreme that they name: `density_weights`: weights are constant zero over exactly a quarter, rounded down, of the 512 x 512 tiles; elsewhere each pixel's weight is drawn afresh.
All inputs are finite; a program needn't handle non-finite values. No bound on the sum of `target_layout` on one device may be relied on, other than what follows from the above.
Results may differ from a plain program's by a relative error of at most 0.001.
Values sent between devices are 32-bit elements; how exact they have to be, the bound alone decides.
A program may use at most 64 MiB of HBM per device.

v0:
```python
import math

import jax
import jax.numpy as jnp
from jax import lax
from jax.sharding import PartitionSpec as P

MARGIN = 128
BAND = 24


STEEPNESS = 6.0
THRESHOLD = 0.25
STEP_SIZE = 4.0


def with_halo(cells, sides, width):
    for axis, dim in sides:
        count = lax.axis_size(axis)
        ends = count - 1
        head = lax.slice_in_dim(cells, 0, width, axis=dim)
        tail = lax.slice_in_dim(cells, cells.shape[dim] - width, cells.shape[dim], axis=dim)
        cells = jnp.concatenate(
            [
                lax.ppermute(tail, axis, [(i, (i + 1) % count) for i in range(ends)]),
                cells,
                lax.ppermute(head, axis, [((i + 1) % count, i) for i in range(ends)]),
            ],
            axis=dim,
        )
    return cells


def matmul_hi(first, second):
    return jnp.dot(
        first, second, precision=lax.Precision.HIGHEST, preferred_element_type=jnp.float32
    )


def contract(form, first, second):
    return jnp.einsum(
        form, first, second, precision=lax.Precision.HIGHEST, preferred_element_type=jnp.float32
    )


def band_tables(count_rows, offset, length, band_size):
    positions = jnp.arange(count_rows, dtype=jnp.int32) + offset
    frequency = jnp.arange(band_size, dtype=jnp.int32) - band_size // 2
    turn_count = jnp.mod(positions[:, None] * frequency[None, :], length).astype(jnp.float32)
    angles = turn_count * (2.0 * math.pi / length)
    return (jnp.cos(angles), jnp.sin(angles))


def spectrum_of(window, band_size):
    length = window.shape[0]
    win_cos, win_sin = band_tables(length, 0, length, band_size)
    normalizer = 1.0 / (length * length)
    projected = matmul_hi(window, jnp.concatenate([win_cos, win_sin], 1))
    proj_cos = projected[:, :band_size]
    proj_sin = projected[:, band_size:]
    spec_re = (matmul_hi(win_cos.T, proj_cos) - matmul_hi(win_sin.T, proj_sin)) * normalizer
    spec_im = -(matmul_hi(win_cos.T, proj_sin) + matmul_hi(win_sin.T, proj_cos)) * normalizer
    return (spec_re, spec_im)


def tile_adjoint(spec_re, spec_im, target_layout, density_weights, kernels_here, length):
    tile_size = target_layout.shape[0]
    band_size = kernels_here.shape[-1]
    margin = (length - tile_size) // 2
    tile_cos, tile_sin = band_tables(tile_size, margin, length, band_size)
    normalizer = 1.0 / (length * length)
    kern_re = kernels_here[:, 0]
    kern_im = kernels_here[:, 1]
    amp_re = kern_re * spec_re - kern_im * spec_im
    amp_im = kern_re * spec_im + kern_im * spec_re
    half_re = contract("kab,tb->kat", amp_re, tile_cos) - contract("kab,tb->kat", amp_im, tile_sin)
    half_im = contract("kab,tb->kat", amp_re, tile_sin) + contract("kab,tb->kat", amp_im, tile_cos)
    right_blocks = jnp.concatenate(
        [jnp.concatenate([half_re, half_im], 2), jnp.concatenate([-half_im, half_re], 2)], 1
    )
    left_block = jnp.concatenate([tile_cos, tile_sin], 1)

    def add_intensity(running, block):
        field_pair = matmul_hi(left_block, block)
        squares = field_pair * field_pair
        return (running + squares[:, :tile_size] + squares[:, tile_size:], None)

    intensity, _ = lax.scan(
        add_intensity, jnp.zeros((tile_size, tile_size), jnp.float32), right_blocks
    )
    resist = jax.nn.sigmoid(STEEPNESS * (intensity - THRESHOLD))
    layout = target_layout.astype(jnp.float32)
    weight_vals = density_weights.astype(jnp.float32)
    intensity_grad = 2.0 * weight_vals * (resist - layout) * STEEPNESS * resist * (1.0 - resist)
    gain_twice = 2.0 * jnp.concatenate([intensity_grad, intensity_grad], 1)

    def adjoint_kernel(block):
        field_pair = matmul_hi(left_block, block)
        adjoint_u = matmul_hi(left_block.T, field_pair * gain_twice)
        grad_re = adjoint_u[:band_size, :tile_size] + adjoint_u[band_size:, tile_size:]
        grad_im = adjoint_u[:band_size, tile_size:] - adjoint_u[band_size:, :tile_size]
        return (grad_re, grad_im)

    u_re, u_im = lax.map(adjoint_kernel, right_blocks)
    za_re = contract("kat,tb->kab", u_re, tile_cos) + contract("kat,tb->kab", u_im, tile_sin)
    za_im = contract("kat,tb->kab", u_im, tile_cos) - contract("kat,tb->kab", u_re, tile_sin)
    zs_re = normalizer * jnp.sum(kern_re * za_re + kern_im * za_im, axis=0)
    zs_im = normalizer * jnp.sum(kern_re * za_im - kern_im * za_re, axis=0)
    return (zs_re, zs_im)


def back_project(zs_re, zs_im, length):
    band_size = zs_re.shape[0]
    win_cos, win_sin = band_tables(length, 0, length, band_size)
    v_re = matmul_hi(zs_re, win_cos.T) - matmul_hi(zs_im, win_sin.T)
    v_im = matmul_hi(zs_re, win_sin.T) + matmul_hi(zs_im, win_cos.T)
    return matmul_hi(jnp.concatenate([win_cos, win_sin], 1), jnp.concatenate([v_re, -v_im], 0))


def per_device(mask_logits, target_layout, density_weights, socs_kernels):
    tile_size = mask_logits.shape[0]
    margin = MARGIN
    band_size = BAND
    length = tile_size + 2 * margin
    mask_now = 0.5 * (1.0 + jnp.tanh(mask_logits))
    kernels_here = socs_kernels[0]
    window = with_halo(mask_now, (("ty", 0), ("tx", 1)), MARGIN)
    spec_re, spec_im = spectrum_of(window, band_size)
    zs_re, zs_im = tile_adjoint(
        spec_re, spec_im, target_layout, density_weights, kernels_here, length
    )
    zs_re, zs_im = lax.psum((zs_re, zs_im), "cond")
    window_grad = back_project(zs_re, zs_im, length)
    side_strips = jnp.concatenate(
        [window_grad[:, :margin], window_grad[:, margin + tile_size :]], 1
    )
    received = with_halo(side_strips, (("tx", 1),), MARGIN)
    center = window_grad[:, margin : margin + tile_size]
    center = center.at[:, :margin].add(received[:, :margin])
    center = center.at[:, tile_size - margin :].add(received[:, 3 * margin :])
    row_strips = jnp.concatenate([center[:margin], center[margin + tile_size :]], 0)
    received_rows = with_halo(row_strips, (("ty", 0),), MARGIN)
    mask_grad = center[margin : margin + tile_size]
    mask_grad = mask_grad.at[:margin].add(received_rows[:margin])
    mask_grad = mask_grad.at[tile_size - margin :].add(received_rows[3 * margin :])
    slope_term = 2.0 * mask_now * (1.0 - mask_now)
    logits_new = mask_logits - STEP_SIZE * mask_grad * slope_term
    mask_next = (0.5 * (1.0 + jnp.tanh(logits_new))).astype(jnp.bfloat16)
    return (logits_new, mask_next)


def solution(mesh):
    in_specs = (P("ty", "tx"), P("ty", "tx"), P("ty", "tx"), P("cond", None, None, None, None))
    out_specs = (P("ty", "tx"), P("ty", "tx"))
    return jax.shard_map(
        per_device, mesh=mesh, in_specs=in_specs, out_specs=out_specs, check_vma=False
    )
```

profile of v0, /device:TPU:1, one launch (start us, length us, event | category | flops | bytes accessed | tf_op | source)
XLA Modules:
  0.0 186.3 jit_solution(7485590320203847725)
XLA Ops:
  2.0 4.0 %collective-permute-start = (f32[128,512]{1,0:T(8,128)S(1)}, f32[128,512]{1,0:T(8,128)S(1)}, u32[]{:S(2)}, u32[]{:S(2)}) collective-permute-start(f32[128,512]{1,0:T(8,128)S(1)} %get-tuple-element.167), channel_id=1, source_target_pairs={{0,4},{1,5},{2,6},{3,7},{8,12},{9,13},{10,14},{11,15},{16,20},{17,... | collective-permute-start | bytes 786440 | tf_op jit(solution)/shard_map/ppermute | solution.py:25
  7.4 3.6 %collective-permute-done = f32[128,512]{1,0:T(8,128)S(1)} collective-permute-done((f32[128,512]{1,0:T(8,128)S(1)}, f32[128,512]{1,0:T(8,128)S(1)}, u32[]{:S(2)}, u32[]{:S(2)}) %collective-permute-start) | collective-permute-done | bytes 262176 | tf_op jit(solution)/shard_map/ppermute | solution.py:25
  11.0 3.8 %collective-permute-done.1 = f32[128,512]{1,0:T(8,128)S(1)} collective-permute-done((f32[128,512]{1,0:T(8,128)S(1)}, f32[128,512]{1,0:T(8,128)S(1)}, u32[]{:S(2)}, u32[]{:S(2)}) %collective-permute-start.1) | collective-permute-done | bytes 262176 | tf_op jit(solution)/shard_map/ppermute | solution.py:27
  14.9 4.8 %collective-permute-start.2 = (f32[768,128]{1,0:T(8,128)S(1)}, f32[768,128]{1,0:T(8,128)}, u32[]{:S(2)}, u32[]{:S(2)}) collective-permute-start(f32[768,128]{1,0:T(8,128)S(1)} %get-tuple-element.165), channel_id=1, source_target_pairs={{0,1},{1,2},{2,3},{4,5},{5,6},{6,7},{8,9},{9,10},{10,11},{12,13},{... | collective-permute-start | bytes 1179656 | tf_op jit(solution)/shard_map/ppermute | solution.py:25
  25.1 3.8 %collective-permute-done.3 = f32[768,128]{1,0:T(8,128)} collective-permute-done((f32[768,128]{1,0:T(8,128)S(1)}, f32[768,128]{1,0:T(8,128)}, u32[]{:S(2)}, u32[]{:S(2)}) %collective-permute-start.3) | collective-permute-done | bytes 393248 | tf_op jit(solution)/shard_map/ppermute | solution.py:27
  28.9 3.5 %fusion.13 = f32[768,48]{0,1:T(8,128)S(1)} fusion(f32[768,128]{1,0:T(8,128)} %collective-permute-done.3, f32[128,512]{1,0:T(8,128)} %copy-done.11, f32[512,512]{1,0:T(8,128)S(1)} %fusion.27, f32[128,512]{1,0:T(8,128)} %copy-done.10, f32[768,128]{1,0:T(8,128)} %collective-permute-done.2, f32[768,24]{0,1:T(8,128)S(1)} %get-tuple-element.172, ...), kind=kOutput, calls=%fused_computation.19 | convolution fusion | flops 342134784 | bytes 2654208 | tf_op jit(solution)/shard_map/dot_general | solution.py:35
  39.9 41.8 %while.28 = (s32[]{:T(128)}, f32[512,512]{0,1:T(8,128)S(1)}, f32[12,48,1024]{2,1,0:T(8,128)}, f32[512,48]{1,0:T(8,128)S(1)}, s32[]{:T(128)}, /*index=5*/s32[]{:T(128)}) while((s32[]{:T(128)}, f32[512,512]{0,1:T(8,128)S(1)}, f32[12,48,1024]{2,1,0:T(8,128)}, f32[512,48]{1,0:T(8,128)S(1)}, s32[]{:T(128)}, /*index=5*/s32[]{:T(128)}) %tuple.70), condition=%wide.region_1.2_spmd.clone, body=%wide.region_0.1_spmd.clone.sunk | while | flops 303300608 | bytes 6586959 | solution.py:88
  39.9 2.8 %multiply_bitcast_fusion.2 = f32[512,1024]{0,1:T(8,128)S(1)} fusion(f32[512,48]{1,0:T(8,128)S(1)} %get-tuple-element.258, f32[12,48,1024]{2,1,0:T(8,128)} %get-tuple-element.257, s32[]{:T(128)} %get-tuple-element.249), kind=kOutput, calls=%fused_computation.13.clone.1 | convolution fusion | flops 302514176 | bytes 2392576 | tf_op jit(solution)/shard_map/while/body/eval_jaxpr/dot_general | solution.py:35
  43.4 2.8 %multiply_bitcast_fusion.2 = f32[512,1024]{0,1:T(8,128)S(1)} fusion(f32[512,48]{1,0:T(8,128)S(1)} %get-tuple-element.258, f32[12,48,1024]{2,1,0:T(8,128)} %get-tuple-element.257, s32[]{:T(128)} %get-tuple-element.249), kind=kOutput, calls=%fused_computation.13.clone.1 | convolution fusion | flops 302514176 | bytes 2392576 | tf_op jit(solution)/shard_map/while/body/eval_jaxpr/dot_general | solution.py:35
  46.9 2.8 %multiply_bitcast_fusion.2 = f32[512,1024]{0,1:T(8,128)S(1)} fusion(f32[512,48]{1,0:T(8,128)S(1)} %get-tuple-element.258, f32[12,48,1024]{2,1,0:T(8,128)} %get-tuple-element.257, s32[]{:T(128)} %get-tuple-element.249), kind=kOutput, calls=%fused_computation.13.clone.1 | convolution fusion | flops 302514176 | bytes 2392576 | tf_op jit(solution)/shard_map/while/body/eval_jaxpr/dot_general | solution.py:35
  50.4 2.8 %multiply_bitcast_fusion.2 = f32[512,1024]{0,1:T(8,128)S(1)} fusion(f32[512,48]{1,0:T(8,128)S(1)} %get-tuple-element.258, f32[12,48,1024]{2,1,0:T(8,128)} %get-tuple-element.257, s32[]{:T(128)} %get-tuple-element.249), kind=kOutput, calls=%fused_computation.13.clone.1 | convolution fusion | flops 302514176 | bytes 2392576 | tf_op jit(solution)/shard_map/while/body/eval_jaxpr/dot_general | solution.py:35
  53.8 2.8 %multiply_bitcast_fusion.2 = f32[512,1024]{0,1:T(8,128)S(1)} fusion(f32[512,48]{1,0:T(8,128)S(1)} %get-tuple-element.258, f32[12,48,1024]{2,1,0:T(8,128)} %get-tuple-element.257, s32[]{:T(128)} %get-tuple-element.249), kind=kOutput, calls=%fused_computation.13.clone.1 | convolution fusion | flops 302514176 | bytes 2392576 | tf_op jit(solution)/shard_map/while/body/eval_jaxpr/dot_general | solution.py:35
  57.3 2.8 %multiply_bitcast_fusion.2 = f32[512,1024]{0,1:T(8,128)S(1)} fusion(f32[512,48]{1,0:T(8,128)S(1)} %get-tuple-element.258, f32[12,48,1024]{2,1,0:T(8,128)} %get-tuple-element.257, s32[]{:T(128)} %get-tuple-element.249), kind=kOutput, calls=%fused_computation.13.clone.1 | convolution fusion | flops 302514176 | bytes 2392576 | tf_op jit(solution)/shard_map/while/body/eval_jaxpr/dot_general | solution.py:35
  60.8 2.8 %multiply_bitcast_fusion.2 = f32[512,1024]{0,1:T(8,128)S(1)} fusion(f32[512,48]{1,0:T(8,128)S(1)} %get-tuple-element.258, f32[12,48,1024]{2,1,0:T(8,128)} %get-tuple-element.257, s32[]{:T(128)} %get-tuple-element.249), kind=kOutput, calls=%fused_computation.13.clone.1 | convolution fusion | flops 302514176 | bytes 2392576 | tf_op jit(solution)/shard_map/while/body/eval_jaxpr/dot_general | solution.py:35
  64.3 2.8 %multiply_bitcast_fusion.2 = f32[512,1024]{0,1:T(8,128)S(1)} fusion(f32[512,48]{1,0:T(8,128)S(1)} %get-tuple-element.258, f32[12,48,1024]{2,1,0:T(8,128)} %get-tuple-element.257, s32[]{:T(128)} %get-tuple-element.249), kind=kOutput, calls=%fused_computation.13.clone.1 | convolution fusion | flops 302514176 | bytes 2392576 | tf_op jit(solution)/shard_map/while/body/eval_jaxpr/dot_general | solution.py:35
  67.8 2.8 %multiply_bitcast_fusion.2 = f32[512,1024]{0,1:T(8,128)S(1)} fusion(f32[512,48]{1,0:T(8,128)S(1)} %get-tuple-element.258, f32[12,48,1024]{2,1,0:T(8,128)} %get-tuple-element.257, s32[]{:T(128)} %get-tuple-element.249), kind=kOutput, calls=%fused_computation.13.clone.1 | convolution fusion | flops 302514176 | bytes 2392576 | tf_op jit(solution)/shard_map/while/body/eval_jaxpr/dot_general | solution.py:35
  71.2 2.8 %multiply_bitcast_fusion.2 = f32[512,1024]{0,1:T(8,128)S(1)} fusion(f32[512,48]{1,0:T(8,128)S(1)} %get-tuple-element.258, f32[12,48,1024]{2,1,0:T(8,128)} %get-tuple-element.257, s32[]{:T(128)} %get-tuple-element.249), kind=kOutput, calls=%fused_computation.13.clone.1 | convolution fusion | flops 302514176 | bytes 2392576 | tf_op jit(solution)/shard_map/while/body/eval_jaxpr/dot_general | solution.py:35
  74.7 2.8 %multiply_bitcast_fusion.2 = f32[512,1024]{0,1:T(8,128)S(1)} fusion(f32[512,48]{1,0:T(8,128)S(1)} %get-tuple-element.258, f32[12,48,1024]{2,1,0:T(8,128)} %get-tuple-element.257, s32[]{:T(128)} %get-tuple-element.249), kind=kOutput, calls=%fused_computation.13.clone.1 | convolution fusion | flops 302514176 | bytes 2392576 | tf_op jit(solution)/shard_map/while/body/eval_jaxpr/dot_general | solution.py:35
  78.2 2.8 %multiply_bitcast_fusion.2 = f32[512,1024]{0,1:T(8,128)S(1)} fusion(f32[512,48]{1,0:T(8,128)S(1)} %get-tuple-element.258, f32[12,48,1024]{2,1,0:T(8,128)} %get-tuple-element.257, s32[]{:T(128)} %get-tuple-element.249), kind=kOutput, calls=%fused_computation.13.clone.1 | convolution fusion | flops 302514176 | bytes 2392576 | tf_op jit(solution)/shard_map/while/body/eval_jaxpr/dot_general | solution.py:35
  85.9 52.1 %while.27 = (s32[]{:T(128)}, f32[12,24,512]{2,1,0:T(8,128)S(1)}, f32[12,24,512]{2,1,0:T(8,128)S(1)}, f32[12,48,1024]{2,1,0:T(8,128)}, f32[512,48]{1,0:T(8,128)S(1)}, /*index=5*/f32[512,1024]{1,0:T(8,128)S(1)}, s32[]{:T(128)}) while((s32[]{:T(128)}, f32[12,24,512]{2,1,0:T(8,128)S(1)}, f32[12,24,512]{2,1,0:T(8,128)S(1)}, ...), condition=%wide.region_3.4_spmd, body=%wide.region_2.3_spmd.sunk | while | flops 604528640 | bytes 7176785 | solution.py:104
  90.2 2.7 %fusion.162 = f32[1024,512]{0,1:T(8,128)S(1)} fusion(f32[512,48]{1,0:T(8,128)S(1)} %get-tuple-element.279, f32[12,48,1024]{2,1,0:T(8,128)} %get-tuple-element.278, s32[]{:T(128)} %get-tuple-element.268), kind=kOutput, calls=%fused_computation.3.clone.1 | convolution fusion | flops 301989888 | bytes 2392576 | tf_op jit(solution)/shard_map/while/body/eval_jaxpr/dot_general | solution.py:35
  94.6 2.7 %fusion.162 = f32[1024,512]{0,1:T(8,128)S(1)} fusion(f32[512,48]{1,0:T(8,128)S(1)} %get-tuple-element.279, f32[12,48,1024]{2,1,0:T(8,128)} %get-tuple-element.278, s32[]{:T(128)} %get-tuple-element.268), kind=kOutput, calls=%fused_computation.3.clone.1 | convolution fusion | flops 301989888 | bytes 2392576 | tf_op jit(solution)/shard_map/while/body/eval_jaxpr/dot_general | solution.py:35
  98.9 2.7 %fusion.162 = f32[1024,512]{0,1:T(8,128)S(1)} fusion(f32[512,48]{1,0:T(8,128)S(1)} %get-tuple-element.279, f32[12,48,1024]{2,1,0:T(8,128)} %get-tuple-element.278, s32[]{:T(128)} %get-tuple-element.268), kind=kOutput, calls=%fused_computation.3.clone.1 | convolution fusion | flops 301989888 | bytes 2392576 | tf_op jit(solution)/shard_map/while/body/eval_jaxpr/dot_general | solution.py:35
  103.3 2.7 %fusion.162 = f32[1024,512]{0,1:T(8,128)S(1)} fusion(f32[512,48]{1,0:T(8,128)S(1)} %get-tuple-element.279, f32[12,48,1024]{2,1,0:T(8,128)} %get-tuple-element.278, s32[]{:T(128)} %get-tuple-element.268), kind=kOutput, calls=%fused_computation.3.clone.1 | convolution fusion | flops 301989888 | bytes 2392576 | tf_op jit(solution)/shard_map/while/body/eval_jaxpr/dot_general | solution.py:35
  107.6 2.7 %fusion.162 = f32[1024,512]{0,1:T(8,128)S(1)} fusion(f32[512,48]{1,0:T(8,128)S(1)} %get-tuple-element.279, f32[12,48,1024]{2,1,0:T(8,128)} %get-tuple-element.278, s32[]{:T(128)} %get-tuple-element.268), kind=kOutput, calls=%fused_computation.3.clone.1 | convolution fusion | flops 301989888 | bytes 2392576 | tf_op jit(solution)/shard_map/while/body/eval_jaxpr/dot_general | solution.py:35
  112.0 2.7 %fusion.162 = f32[1024,512]{0,1:T(8,128)S(1)} fusion(f32[512,48]{1,0:T(8,128)S(1)} %get-tuple-element.279, f32[12,48,1024]{2,1,0:T(8,128)} %get-tuple-element.278, s32[]{:T(128)} %get-tuple-element.268), kind=kOutput, calls=%fused_computation.3.clone.1 | convolution fusion | flops 301989888 | bytes 2392576 | tf_op jit(solution)/shard_map/while/body/eval_jaxpr/dot_general | solution.py:35
  116.3 2.7 %fusion.162 = f32[1024,512]{0,1:T(8,128)S(1)} fusion(f32[512,48]{1,0:T(8,128)S(1)} %get-tuple-element.279, f32[12,48,1024]{2,1,0:T(8,128)} %get-tuple-element.278, s32[]{:T(128)} %get-tuple-element.268), kind=kOutput, calls=%fused_computation.3.clone.1 | convolution fusion | flops 301989888 | bytes 2392576 | tf_op jit(solution)/shard_map/while/body/eval_jaxpr/dot_general | solution.py:35
  133.7 2.7 %fusion.162 = f32[1024,512]{0,1:T(8,128)S(1)} fusion(f32[512,48]{1,0:T(8,128)S(1)} %get-tuple-element.279, f32[12,48,1024]{2,1,0:T(8,128)} %get-tuple-element.278, s32[]{:T(128)} %get-tuple-element.268), kind=kOutput, calls=%fused_computation.3.clone.1 | convolution fusion | flops 301989888 | bytes 2392576 | tf_op jit(solution)/shard_map/while/body/eval_jaxpr/dot_general | solution.py:35
  141.5 15.5 %all-reduce = (f32[24,24]{1,0:T(8,128)S(1)}, f32[24,24]{1,0:T(8,128)S(1)}) all-reduce(f32[24,24]{1,0:T(8,128)S(1)} %get-tuple-element.176, f32[24,24]{1,0:T(8,128)S(1)} %get-tuple-element.175), channel_id=1, replica_groups=mesh['cond'=4,'ty'=2,'tx'=4] {'cond'}, use_global_device_ids=true, to_apply=%region_5.6 | all-reduce | flops 1152 | bytes 9216 | tf_op jit(solution)/shard_map/psum | solution.py:132
  161.3 5.4 %collective-permute-start.4 = (f32[768,128]{1,0:T(8,128)S(1)}, f32[768,128]{1,0:T(8,128)S(1)}, u32[]{:S(2)}, u32[]{:S(2)}) collective-permute-start(f32[768,128]{1,0:T(8,128)S(1)} %get-tuple-element.162), channel_id=1, source_target_pairs={{0,1},{1,2},{2,3},{4,5},{5,6},{6,7},{8,9},{9,10},{10,11},{12,13},{... | collective-permute-start | bytes 1179656 | tf_op jit(solution)/shard_map/ppermute | solution.py:25
  172.1 3.7 %collective-permute-done.5 = f32[768,128]{1,0:T(8,128)S(1)} collective-permute-done((f32[768,128]{1,0:T(8,128)S(1)}, f32[768,128]{1,0:T(8,128)S(1)}, u32[]{:S(2)}, u32[]{:S(2)}) %collective-permute-start.5) | collective-permute-done | bytes 393248 | tf_op jit(solution)/shard_map/ppermute | solution.py:27
  180.9 3.8 %collective-permute-done.7 = f32[128,512]{1,0:T(8,128)S(1)} collective-permute-done((f32[128,512]{1,0:T(8,128)S(1)}, f32[128,512]{1,0:T(8,128)S(1)}, u32[]{:S(2)}, u32[]{:S(2)}) %collective-permute-start.7) | collective-permute-done | bytes 262176 | tf_op jit(solution)/shard_map/ppermute | solution.py:27
  (117 shorter events, 77.4 us)
Async XLA Ops:
  2.0 8.9 %collective-permute-start = (f32[128,512]{1,0:T(8,128)S(1)}, f32[128,512]{1,0:T(8,128)S(1)}, u32[]{:S(2)}, u32[]{:S(2)}) collective-permute-start(f32[128,512]{1,0:T(8,128)S(1)} %get-tuple-element.167), channel_id=1, source_target_pairs={{0,4},{1,5},{2,6},{3,7},{8,12},{9,13},{10,14},{11,15},{16,20},{17,... | collective-permute-start | bytes 786440 | tf_op jit(solution)/shard_map/ppermute | solution.py:25
  6.0 8.8 %collective-permute-start.1 = (f32[128,512]{1,0:T(8,128)S(1)}, f32[128,512]{1,0:T(8,128)S(1)}, u32[]{:S(2)}, u32[]{:S(2)}) collective-permute-start(f32[128,512]{1,0:T(8,128)S(1)} %get-tuple-element.168), channel_id=1, source_target_pairs={{4,0},{5,1},{6,2},{7,3},{12,8},{13,9},{14,10},{15,11},{20,16},{21,... | collective-permute-start | bytes 786440 | tf_op jit(solution)/shard_map/ppermute | solution.py:27
  11.0 11.6 %copy-start.10 = (f32[128,512]{1,0:T(8,128)}, f32[128,512]{1,0:T(8,128)S(1)}, u32[]{:S(2)}) copy-start(f32[128,512]{1,0:T(8,128)S(1)} %collective-permute-done) | copy-start | bytes 786436
  14.8 8.8 %copy-start.11 = (f32[128,512]{1,0:T(8,128)}, f32[128,512]{1,0:T(8,128)S(1)}, u32[]{:S(2)}) copy-start(f32[128,512]{1,0:T(8,128)S(1)} %collective-permute-done.1) | copy-start | bytes 786436
  14.9 10.2 %collective-permute-start.2 = (f32[768,128]{1,0:T(8,128)S(1)}, f32[768,128]{1,0:T(8,128)}, u32[]{:S(2)}, u32[]{:S(2)}) collective-permute-start(f32[768,128]{1,0:T(8,128)S(1)} %get-tuple-element.165), channel_id=1, source_target_pairs={{0,1},{1,2},{2,3},{4,5},{5,6},{6,7},{8,9},{9,10},{10,11},{12,13},{... | collective-permute-start | bytes 1179656 | tf_op jit(solution)/shard_map/ppermute | solution.py:25
  19.7 9.2 %collective-permute-start.3 = (f32[768,128]{1,0:T(8,128)S(1)}, f32[768,128]{1,0:T(8,128)}, u32[]{:S(2)}, u32[]{:S(2)}) collective-permute-start(f32[768,128]{1,0:T(8,128)S(1)} %get-tuple-element.166), channel_id=1, source_target_pairs={{1,0},{2,1},{3,2},{5,4},{6,5},{7,6},{9,8},{10,9},{11,10},{13,12},{... | collective-permute-start | bytes 1179656 | tf_op jit(solution)/shard_map/ppermute | solution.py:27
  23.6 13.8 %copy-start.1 = (f32[1,12,2,24,24]{4,3,1,2,0:T(8,128)}, f32[1,12,2,24,24]{4,3,1,2,0:T(8,128)S(1)}, u32[]{:S(2)}) copy-start(f32[1,12,2,24,24]{4,3,1,2,0:T(8,128)S(1)} %copy.21) | copy-start | bytes 165892
  25.1 7.4 %copy-start.6 = (f32[768,24]{0,1:T(8,128)}, f32[768,24]{0,1:T(8,128)S(1)}, u32[]{:S(2)}) copy-start(f32[768,24]{0,1:T(8,128)S(1)} %get-tuple-element.171) | copy-start | bytes 221188
  25.1 7.4 %copy-start.8 = (f32[768,24]{0,1:T(8,128)}, f32[768,24]{0,1:T(8,128)S(1)}, u32[]{:S(2)}) copy-start(f32[768,24]{0,1:T(8,128)S(1)} %get-tuple-element.172) | copy-start | bytes 221188
  81.7 1.2 copy-start.5
  84.7 1.1 copy-start.3
  84.7 1.2 copy-start.4
  138.0 2.6 %copy-start.2 = (f32[1,12,2,24,24]{4,3,1,2,0:T(8,128)S(1)}, f32[1,12,2,24,24]{4,3,1,2,0:T(8,128)}, u32[]{:S(2)}) copy-start(f32[1,12,2,24,24]{4,3,1,2,0:T(8,128)} %copy-done.1) | copy-start | bytes 165892
  138.0 21.1 %copy-start.7 = (f32[768,24]{0,1:T(8,128)S(1)}, f32[768,24]{0,1:T(8,128)}, u32[]{:S(2)}) copy-start(f32[768,24]{0,1:T(8,128)} %copy-done.6) | copy-start | bytes 221188
  138.1 21.1 %copy-start.9 = (f32[768,24]{0,1:T(8,128)S(1)}, f32[768,24]{0,1:T(8,128)}, u32[]{:S(2)}) copy-start(f32[768,24]{0,1:T(8,128)} %copy-done.8) | copy-start | bytes 221188
  161.3 10.1 %collective-permute-start.4 = (f32[768,128]{1,0:T(8,128)S(1)}, f32[768,128]{1,0:T(8,128)S(1)}, u32[]{:S(2)}, u32[]{:S(2)}) collective-permute-start(f32[768,128]{1,0:T(8,128)S(1)} %get-tuple-element.162), channel_id=1, source_target_pairs={{0,1},{1,2},{2,3},{4,5},{5,6},{6,7},{8,9},{9,10},{10,11},{12,13},{... | collective-permute-start | bytes 1179656 | tf_op jit(solution)/shard_map/ppermute | solution.py:25
  166.7 9.1 %collective-permute-start.5 = (f32[768,128]{1,0:T(8,128)S(1)}, f32[768,128]{1,0:T(8,128)S(1)}, u32[]{:S(2)}, u32[]{:S(2)}) collective-permute-start(f32[768,128]{1,0:T(8,128)S(1)} %get-tuple-element.161), channel_id=1, source_target_pairs={{1,0},{2,1},{3,2},{5,4},{6,5},{7,6},{9,8},{10,9},{11,10},{13,12},{... | collective-permute-start | bytes 1179656 | tf_op jit(solution)/shard_map/ppermute | solution.py:27
  176.0 8.8 %copy-start = (f32[512,512]{1,0:T(8,128)S(1)}, f32[512,512]{1,0:T(8,128)}, u32[]{:S(2)}) copy-start(f32[512,512]{1,0:T(8,128)} %param.16) | copy-start | bytes 3145732
  176.0 4.9 %collective-permute-start.6 = (f32[128,512]{1,0:T(8,128)S(1)}, f32[128,512]{1,0:T(8,128)S(1)}, u32[]{:S(2)}, u32[]{:S(2)}) collective-permute-start(f32[128,512]{1,0:T(8,128)S(1)} %get-tuple-element.164), channel_id=1, source_target_pairs={{0,4},{1,5},{2,6},{3,7},{8,12},{9,13},{10,14},{11,15},{16,20},{17,... | collective-permute-start | bytes 786440 | tf_op jit(solution)/shard_map/ppermute | solution.py:25
  177.6 7.1 %collective-permute-start.7 = (f32[128,512]{1,0:T(8,128)S(1)}, f32[128,512]{1,0:T(8,128)S(1)}, u32[]{:S(2)}, u32[]{:S(2)}) collective-permute-start(f32[128,512]{1,0:T(8,128)S(1)} %get-tuple-element.163), channel_id=1, source_target_pairs={{4,0},{5,1},{6,2},{7,3},{12,8},{13,9},{14,10},{15,11},{20,16},{21,... | collective-permute-start | bytes 786440 | tf_op jit(solution)/shard_map/ppermute | solution.py:27
where the time goes:
time: 188 us; the launch traced here: 186 us
  matrix products  102 us (54%)
  waiting for transfers between devices  22.7 us (12%)
  starting transfers between devices  22.2 us (12%)
  other arithmetic  18.7 us (10%)
  blocking collectives  15.5 us (8%)
  local copies, waits for them, and re-layouts  3.78 us (2%)
    dot_general x46, matrix products, matmul_hi(): jnp.dot(first, second, precision=lax.Precision.HIGHEST, preferred_element...  94.8 us
    ppermute x4, starting transfers between devices, with_halo(): lax.ppermute(tail, axis, [(i, (i + 1) % count) for i in range(ends)])  15.8 us
    psum x1, blocking collectives, per_device(): zs_re, zs_im = lax.psum((zs_re, zs_im), 'cond')  15.5 us
    ppermute x4, waiting for transfers between devices, with_halo(): lax.ppermute(head, axis, [((i + 1) % count, i) for i in range(ends)])  15.2 us
    add x12, other arithmetic, add_intensity(): return (running + squares[:, :tile_size] + squares[:, tile_size:], None)  8.12 us
    ppermute x4, waiting for transfers between devices, with_halo(): lax.ppermute(tail, axis, [(i, (i + 1) % count) for i in range(ends)])  7.49 us
    dot_general x8, matrix products, contract(): jnp.einsum(form, first, second, precision=lax.Precision.HIGHEST, preferre...  6.81 us
    ppermute x4, starting transfers between devices, with_halo(): lax.ppermute(head, axis, [((i + 1) % count, i) for i in range(ends)])  6.43 us
  transfers between devices with their start and end apart: 8, of which 7 were waited for; matrix products, arithmetic and copies ran while one was open for 3% of the time, Pallas kernels for 0%

commit v1 on v0

v1 whole, which is shorter than its diff:
```python
import functools
import math

import jax
import jax.numpy as jnp
import numpy as np
from jax import lax
from jax.experimental import pallas as pl
from jax.experimental.pallas import tpu as pltpu
from jax.sharding import PartitionSpec as P

MARGIN = 128
BAND = 24
STEEPNESS = 6.0
THRESHOLD = 0.25
STEP_SIZE = 4.0
LANES = 128
MESH = pl.DeviceIdType.MESH
OFFSETS = [(dr, dc) for dr in (-1, 0, 1) for dc in (-1, 0, 1)]
BF = jnp.bfloat16
F32 = jnp.float32


def waves(positions, frequency, period):
    turns = np.mod(np.outer(positions, frequency), period).astype(np.float64)
    return np.cos(turns * (2 * math.pi / period)), np.sin(turns * (2 * math.pi / period))


def halves(table):
    table = np.asarray(table, np.float32)
    high = table.astype(BF)
    return high, (table - high.astype(np.float32)).astype(BF)


def place(rows, cols, *pieces):
    out = np.zeros((rows, cols))
    for top, left, piece in pieces:
        out[top : top + piece.shape[0], left : left + piece.shape[1]] = piece
    return out


def make_tables(tile, margin, band):
    length = tile + 2 * margin
    norm = 1.0 / (length * length)
    freq = np.arange(band) - band // 2
    grid = -(-(2 * band - 1) // 16) * 16
    shifted = []
    for step in (-1, 0, 1):
        spots = np.arange(tile) + margin - step * tile
        inside = ((spots >= 0) & (spots < length))[:, None]
        cos, sin = waves(spots, freq, length)
        shifted.append((cos * inside, sin * inside))
    col_cos = np.concatenate([c for c, _ in shifted], 1)
    col_sin = np.concatenate([s for _, s in shifted], 1)
    fwd_cols = place(tile, 2 * LANES, (0, 0, col_cos), (0, LANES, col_sin))
    fwd_rows = norm * np.concatenate(
        [np.block([[c.T, -s.T], [-s.T, -c.T]]) for c, s in shifted], 0
    )
    ec, es = waves(np.arange(grid), freq, grid)
    right_re = place(LANES, 2 * LANES, (0, 0, ec.T), (0, LANES, es.T))
    right_im = place(LANES, 2 * LANES, (0, 0, -es.T), (0, LANES, ec.T))
    left = np.block([[ec, -es], [es, ec]])
    right_back = place(
        2 * LANES, 2 * LANES,
        (0, 0, ec), (0, LANES, -es), (LANES, 0, es), (LANES, LANES, ec),
    )
    orders = np.arange(1, band)
    turn = (np.arange(tile) + margin)[:, None] / length - np.arange(grid)[None, :] / grid
    interp = (1 + 2 * np.cos(2 * math.pi * turn[:, :, None] * orders).sum(-1)) / grid
    ih, il = halves(interp)
    lh, ll = halves(left)
    th, tl = halves(left.T)
    ih128 = place(tile, LANES, (0, 0, ih.astype(np.float64)))
    il128 = place(tile, LANES, (0, 0, il.astype(np.float64)))
    back_rows = np.concatenate([np.concatenate([c, -s], 1) for c, s in shifted], 1)
    bh, bl = halves(back_rows)
    back_cols = place(LANES, 2 * tile, (0, 0, col_cos.T), (0, tile, col_sin.T))
    front = dict(
        fch=halves(fwd_cols)[0], fcl=halves(fwd_cols)[1],
        frh=halves(fwd_rows)[0], frl=halves(fwd_rows)[1],
        rrh=halves(right_re)[0], rrl=halves(right_re)[1],
        rih=halves(right_im)[0], ril=halves(right_im)[1],
        left=np.concatenate([lh, lh, ll], 1),
        wth=ih128.T.astype(BF), wtl=il128.T.astype(BF),
        wcat=np.concatenate([ih, ih, il], 1),
        wn=np.concatenate([ih128, il128], 1).astype(BF),
        lt=np.concatenate([th, th, tl], 1),
        rbh=halves(right_back)[0], rbl=halves(right_back)[1],
    )
    back = dict(
        bch=halves(back_cols)[0], bcl=halves(back_cols)[1],
        brow=np.concatenate([bh, bh, bl], 1),
    )
    return front, back, grid


def split(x):
    high = x.astype(BF)
    return high, (x - high.astype(F32)).astype(BF)


def mm(a, b):
    return jnp.dot(a, b, preferred_element_type=F32)


def mm3(ah, al, bh, bl):
    return mm(ah, bh) + mm(ah, bl) + mm(al, bh)


def front_kernel(names, grid, n_k, *refs):
    n_tab = len(names)
    logits_hbm, target_hbm, weight_hbm, kern_hbm = refs[:4]
    tab_hbm = dict(zip(names, refs[4 : 4 + n_tab]))
    out_ref = refs[4 + n_tab]
    rest = refs[5 + n_tab :]
    logits, target, weight, kern = rest[:4]
    tab = dict(zip(names, rest[4 : 4 + n_tab]))
    (kpad, send1, recv1, zs_own, recv_c, zs_sum, recv2,
     load_sem, s1, r1, sc, rc, s2, r2) = rest[4 + n_tab :]

    tile = logits.shape[0]
    band = kern.shape[-1]
    both = 2 * band
    length = tile + 2 * MARGIN
    norm = 1.0 / (length * length)
    n_ty, n_tx, n_c = lax.axis_size("ty"), lax.axis_size("tx"), lax.axis_size("cond")
    ty, tx, me = lax.axis_index("ty"), lax.axis_index("tx"), lax.axis_index("cond")

    loads = {}
    order = ["logits", "fch", "fcl", "frh", "frl", "kern"]
    order += [n for n in names if n not in order] + ["target", "weight"]
    src = dict(tab_hbm, logits=logits_hbm, target=target_hbm, weight=weight_hbm, kern=kern_hbm)
    dst = dict(tab, logits=logits, target=target, weight=weight, kern=kern)
    for i, name in enumerate(order):
        loads[name] = pltpu.make_async_copy(src[name], dst[name], load_sem.at[i])
        loads[name].start()

    def exists(dr, dc):
        row, col = ty + dr, tx + dc
        return (row >= 0) & (row < n_ty) & (col >= 0) & (col < n_tx)

    around = [(i, o) for i, o in enumerate(OFFSETS) if o != (0, 0)]
    barrier = pltpu.get_barrier_semaphore()
    for _, (dr, dc) in around:
        @pl.when(exists(dr, dc))
        def _():
            pl.semaphore_signal(
                barrier, inc=1, device_id={"ty": ty + dr, "tx": tx + dc}, device_id_type=MESH
            )
    for j in range(1, n_c):
        pl.semaphore_signal(
            barrier, inc=1, device_id={"cond": lax.rem(me + j, n_c)}, device_id_type=MESH
        )
    for i, (dr, dc) in around:
        @pl.when(jnp.logical_not(exists(-dr, -dc)))
        def _():
            recv1[i] = jnp.zeros(recv1.shape[1:], F32)
            recv2[i] = jnp.zeros(recv2.shape[1:], F32)
    kpad[...] = jnp.zeros(kpad.shape, F32)

    loads["logits"].wait()
    loads["fch"].wait()
    loads["fcl"].wait()
    mask = 0.5 * (1.0 + jnp.tanh(logits[...]))
    mh, ml = split(mask)
    fch = tab["fch"][...]
    proj = mm(mh, fch) + mm(ml, fch) + mm(mh, tab["fcl"][...])
    ph, pw = split(jnp.concatenate([proj[:, :LANES], proj[:, LANES:]], 0))
    loads["frh"].wait()
    loads["frl"].wait()
    share = mm3(tab["frh"][...], tab["frl"][...], ph, pw)
    for i, (dr, dc) in enumerate(OFFSETS):
        rows = share[(dr + 1) * both : (dr + 2) * both]
        send1[i] = rows if dc == -1 else pltpu.roll(rows, LANES - (dc + 1) * band, 1)

    peers = n_c - 1
    for _, (dr, dc) in around:
        peers = peers + exists(dr, dc).astype(jnp.int32)
    pl.semaphore_wait(barrier, peers)

    def to_neighbour(source, dest, ss, rs, i, dr, dc):
        return pltpu.make_async_remote_copy(
            src_ref=source, dst_ref=dest.at[i], send_sem=ss.at[i], recv_sem=rs.at[i],
            device_id={"ty": ty + dr, "tx": tx + dc}, device_id_type=MESH,
        )

    for i, (dr, dc) in around:
        @pl.when(exists(dr, dc))
        def _():
            to_neighbour(send1.at[i], recv1, s1, r1, i, dr, dc).start()
    loads["kern"].wait()
    kpad[:, :, :, :band] = kern[0]
    for name in order:
        if name not in ("logits", "fch", "fcl", "frh", "frl", "kern"):
            loads[name].wait()
    spec = send1[4]
    for i, (dr, dc) in around:
        @pl.when(exists(-dr, -dc))
        def _():
            to_neighbour(send1.at[i], recv1, s1, r1, i, dr, dc).wait_recv()
    for i, _ in around:
        spec = spec + recv1[i]

    sr, si = spec[:band], spec[band:]
    kr, ki = kpad[:, 0], kpad[:, 1]
    ar = (kr * sr - ki * si).reshape(n_k * band, LANES)
    ai = (kr * si + ki * sr).reshape(n_k * band, LANES)
    arh, arl = split(ar)
    aih, ail = split(ai)
    half = mm3(arh, arl, tab["rrh"][...], tab["rrl"][...]) + mm3(
        aih, ail, tab["rih"][...], tab["ril"][...]
    )
    stacked = jnp.concatenate(
        [
            jnp.concatenate(
                [
                    half[k * band : (k + 1) * band, :LANES],
                    half[k * band : (k + 1) * band, LANES:],
                ],
                0,
            )
            for k in range(n_k)
        ],
        1,
    )
    hh, hl = split(stacked)
    field = mm(tab["left"][...], jnp.concatenate([hh, hl, hh], 0))
    squares = field * field
    coarse = jnp.zeros((grid, LANES), F32)
    for k in range(n_k):
        cut = squares[:, k * LANES : (k + 1) * LANES]
        coarse = coarse + cut[:grid] + cut[grid:]
    ch, cl = split(coarse)
    uh, ul = split(mm3(ch, cl, tab["wth"][...], tab["wtl"][...]))
    ustack = jnp.concatenate([uh, ul, uh], 0)

    wn = tab["wn"][...]
    chunk = min(tile, 128)
    col_parts = []
    for row in range(0, tile, chunk):
        intensity = mm(tab["wcat"][row : row + chunk], ustack)
        th = jnp.tanh((0.5 * STEEPNESS) * (intensity - THRESHOLD))
        resist = 0.5 + 0.5 * th
        layout = target[row : row + chunk].astype(F32)
        vals = weight[row : row + chunk].astype(F32)
        gain = (STEEPNESS * 2.0) * vals * (resist - layout) * resist * (1.0 - resist)
        gh, gl = split(gain)
        wide = mm(gh, wn)
        col_parts.append(wide[:, :LANES] + wide[:, LANES:] + mm(gl, wn[:, :LANES]))
    yh, yl = split(jnp.concatenate(col_parts, 0))
    gcoarse = 2.0 * mm3(tab["wth"][:grid], tab["wtl"][:grid], yh, yl)

    gpair = jnp.concatenate([gcoarse, gcoarse], 0)
    slope = jnp.concatenate(
        [gpair * field[:, k * LANES : (k + 1) * LANES] for k in range(n_k)], 1
    )
    dh, dl = split(slope)
    u = mm(tab["lt"][...], jnp.concatenate([dh, dl, dh], 0))
    uu = jnp.concatenate(
        [
            jnp.concatenate(
                [
                    u[:band, k * LANES : (k + 1) * LANES],
                    u[band:, k * LANES : (k + 1) * LANES],
                ],
                1,
            )
            for k in range(n_k)
        ],
        0,
    )
    vh, vl = split(uu)
    za = mm3(vh, vl, tab["rbh"][...], tab["rbl"][...])
    za_re = za[:, :LANES].reshape(n_k, band, LANES)
    za_im = za[:, LANES:].reshape(n_k, band, LANES)
    zs_own[:band] = norm * jnp.sum(kr * za_re + ki * za_im, axis=0)
    zs_own[band:] = norm * jnp.sum(kr * za_im - ki * za_re, axis=0)

    over = []
    for j in range(1, n_c):
        copy = pltpu.make_async_remote_copy(
            src_ref=zs_own, dst_ref=recv_c.at[j], send_sem=sc.at[j], recv_sem=rc.at[j],
            device_id={"cond": lax.rem(me + j, n_c)}, device_id_type=MESH,
        )
        copy.start()
        over.append(copy)
    total = zs_own[...]
    for j, copy in enumerate(over):
        copy.wait_recv()
        total = total + recv_c[j + 1]
    zs_sum[...] = total
    for i, (dr, dc) in around:
        @pl.when(exists(dr, dc))
        def _():
            to_neighbour(zs_sum, recv2, s2, r2, i, dr, dc).start()
    recv2[4] = total
    for i, (dr, dc) in around:
        @pl.when(exists(-dr, -dc))
        def _():
            to_neighbour(zs_sum, recv2, s2, r2, i, dr, dc).wait_recv()
    for er in (-1, 0, 1):
        acc = jnp.zeros((both, LANES), F32)
        for ec in (-1, 0, 1):
            block = recv2[OFFSETS.index((-er, -ec))]
            acc = acc + (block if ec == -1 else pltpu.roll(block, (ec + 1) * band, 1))
        out_ref[(er + 1) * both : (er + 2) * both] = acc

    for i, (dr, dc) in around:
        @pl.when(exists(dr, dc))
        def _():
            to_neighbour(send1.at[i], recv1, s1, r1, i, dr, dc).wait_send()
            to_neighbour(zs_sum, recv2, s2, r2, i, dr, dc).wait_send()
    for copy in over:
        copy.wait_send()


def back_kernel(band, z_ref, bch, bcl, brow, logits, new_ref, next_ref, stack):
    tile = logits.shape[1]
    both = 2 * band

    @pl.when(pl.program_id(0) == 0)
    def _():
        zh, zl = split(z_ref[...])
        wide = mm3(zh, zl, bch[...], bcl[...])
        rows = []
        for a in range(3):
            re = wide[a * both : a * both + band]
            im = wide[a * both + band : (a + 1) * both]
            rows += [re[:, :tile] - im[:, tile:], re[:, tile:] + im[:, :tile]]
        vh, vl = split(jnp.concatenate(rows, 0))
        n = 3 * both
        stack[:n] = vh
        stack[n : 2 * n] = vl
        stack[2 * n :] = vh

    grad = mm(brow[...], stack[...])
    x = logits[...]
    mask = 0.5 * (1.0 + jnp.tanh(x))
    new = x - STEP_SIZE * grad * (2.0 * mask * (1.0 - mask))
    new_ref[...] = new
    next_ref[...] = (0.5 * (1.0 + jnp.tanh(new))).astype(BF)


def per_device(mask_logits, target_layout, density_weights, socs_kernels):
    tile = mask_logits.shape[0]
    band = socs_kernels.shape[-1]
    n_k = socs_kernels.shape[1]
    n_c = lax.axis_size("cond")
    front, back, grid = make_tables(tile, MARGIN, band)
    names = list(front)
    both = 2 * band
    arrays = [mask_logits, target_layout, density_weights, socs_kernels]
    arrays += [jnp.asarray(front[n]) for n in names]
    dma = pltpu.SemaphoreType.DMA
    n_off = len(OFFSETS)
    zrow = pl.pallas_call(
        functools.partial(front_kernel, names, grid, n_k),
        out_shape=jax.ShapeDtypeStruct((3 * both, LANES), F32),
        in_specs=[pl.BlockSpec(memory_space=pl.ANY)] * len(arrays),
        out_specs=pl.BlockSpec(memory_space=pltpu.VMEM),
        scratch_shapes=[pltpu.VMEM(a.shape, a.dtype) for a in arrays]
        + [
            pltpu.VMEM((n_k, 2, band, LANES), F32),
            pltpu.VMEM((n_off, both, LANES), F32),
            pltpu.VMEM((n_off, both, LANES), F32),
            pltpu.VMEM((both, LANES), F32),
            pltpu.VMEM((n_c, both, LANES), F32),
            pltpu.VMEM((both, LANES), F32),
            pltpu.VMEM((n_off, both, LANES), F32),
            dma((len(arrays),)),
            dma((n_off,)),
            dma((n_off,)),
            dma((n_c,)),
            dma((n_c,)),
            dma((n_off,)),
            dma((n_off,)),
        ],
        compiler_params=pltpu.CompilerParams(
            collective_id=0, has_side_effects=True, vmem_limit_bytes=60 * 2**20
        ),
    )(*arrays)

    blocks = 4
    rows = tile // blocks
    whole = lambda shape: pl.BlockSpec(shape, lambda i: (0, 0))
    by_row = lambda width: pl.BlockSpec((rows, width), lambda i: (i, 0))
    return pl.pallas_call(
        functools.partial(back_kernel, band),
        grid=(blocks,),
        out_shape=(
            jax.ShapeDtypeStruct((tile, tile), F32),
            jax.ShapeDtypeStruct((tile, tile), BF),
        ),
        in_specs=[
            whole((3 * both, LANES)),
            whole(back["bch"].shape),
            whole(back["bcl"].shape),
            by_row(back["brow"].shape[1]),
            by_row(tile),
        ],
        out_specs=(by_row(tile), by_row(tile)),
        scratch_shapes=[pltpu.VMEM((9 * both, tile), BF)],
    )(zrow, jnp.asarray(back["bch"]), jnp.asarray(back["bcl"]), jnp.asarray(back["brow"]), mask_logits)


def solution(mesh):
    in_specs = (P("ty", "tx"), P("ty", "tx"), P("ty", "tx"), P("cond", None, None, None, None))
    out_specs = (P("ty", "tx"), P("ty", "tx"))
    return jax.shard_map(
        per_device, mesh=mesh, in_specs=in_specs, out_specs=out_specs, check_vma=False
    )
```

time: 188 us -> 25.7 us (0.14)
  matrix products: 102 us -> 0 us
  Pallas kernels: 0 us -> 24.8 us
  waiting for transfers between devices: 22.7 us -> 0 us
  starting transfers between devices: 22.2 us -> 0 us
  other arithmetic: 18.7 us -> 0 us
  blocking collectives: 15.5 us -> 0 us
  local copies, waits for them, and re-layouts: 3.78 us -> 0 us
    dot_general x54 -> x0, matrix products: 102 us -> none  [the longest x46 94.8 us: matmul_hi(): jnp.dot(first, second, precision=lax.Precision.HIGHEST, preferred_element...]
    pallas_call x0 -> x2, Pallas kernels: none -> 24.8 us  [the longest x1 20.2 us: per_device(): pl.pallas_call(functools.partial(front_kernel, names, grid, n_k), out_sha...]
    ppermute x8 -> x0, waiting for transfers between devices: 22.7 us -> none  [the longest x4 15.2 us: with_halo(): lax.ppermute(head, axis, [((i + 1) % count, i) for i in range(ends)])]
    ppermute x8 -> x0, starting transfers between devices: 22.2 us -> none  [the longest x4 15.8 us: with_halo(): lax.ppermute(tail, axis, [(i, (i + 1) % count) for i in range(ends)])]
    psum x1 -> x0, blocking collectives: 15.5 us -> none  [per_device(): zs_re, zs_im = lax.psum((zs_re, zs_im), 'cond')]
    add x13 -> x0, other arithmetic: 8.13 us -> none  [the longest x12 8.12 us: add_intensity(): return (running + squares[:, :tile_size] + squares[:, tile_size:], None)]
    mul x4 -> x0, other arithmetic: 3.3 us -> none  [the longest x1 1.74 us: tile_adjoint(): 2.0 * weight_vals * (resist - layout) * STEEPNESS * resist * (1.0 - resist)]
    unnamed x25 -> x0, local copies, waits for them, and re-layouts: 2.95 us -> none
  transfers between devices with their start and end apart: 8 -> 0, of which waited for: 7 -> 0; matrix products, arithmetic and copies ran while one was open for 3% -> 0% of each run, Pallas kernels for 0% -> 0%
where the time goes in v1:
time: 25.7 us; the launch traced here: 25.5 us
  Pallas kernels  24.8 us (96%)
  between operations  0.64 us (2%)
    pallas_call x1, Pallas kernels, per_device(): pl.pallas_call(functools.partial(front_kernel, names, grid, n_k), out_sha...  20.2 us
    pallas_call x1, Pallas kernels, per_device(): pl.pallas_call(functools.partial(back_kernel, band), grid=(blocks,), out_...  4.66 us

profile of v1, /device:TPU:1, one launch (start us, length us, event | category | flops | bytes accessed | tf_op | source)
XLA Modules:
  0.0 25.5 jit_solution(14256683404164224736)
XLA Ops:
  0.6 20.2 %shard_map.230.z_ref = f32[144,128]{1,0:T(8,128)} custom-call(f32[512,512]{1,0:T(8,128)} %logits.1, s32[512,512]{1,0:T(8,128)} %refs_1_.1, s32[512,512]{1,0:T(8,128)} %refs_2_.1, f32[1,12,2,24,24]{4,3,2,1,0:T(8,128)} %refs_3_.1, bf16[512,256]{1,0:T(8,128)(2,1)} %constant.38.clone.refs_4_, bf16[512,256]{1,0:T(8,128)(2,1)} %constant.39.clone.refs_5_, ...), custom_call_target="tpu_custom_call" | custom-call | tf_op jit(solution)/shard_map/pallas_call | solution.py:356
  20.8 4.7 %shard_map.231 = (f32[512,512]{1,0:T(8,128)}, bf16[512,512]{1,0:T(8,128)(2,1)}) custom-call(f32[144,128]{1,0:T(8,128)} %shard_map.230.z_ref, bf16[128,1024]{1,0:T(8,128)(2,1)} %constant.54.clone.bch, bf16[128,1024]{1,0:T(8,128)(2,1)} %constant.55.clone.bcl, bf16[512,432]{1,0:T(8,128)(2,1)} %constant.56.clone.brow, f32[512,512]{1,0:T(8,128)} %logits.1), custom_call_target="tpu_custom_call" | custom-call | tf_op jit(solution)/shard_map/pallas_call | solution.py:387

commit v2 on v1

--- a/solution.py
+++ b/solution.py
@@ -107,16 +107,59 @@
     return mm(ah, bh) + mm(ah, bl) + mm(al, bh)
 
 
+def roll(x, shift):
+    shift = shift % LANES
+    return x if shift == 0 else pltpu.roll(x, shift, 1)
+
+
+def packing(band):
+    groups = 2 * band // 8
+    count = -(-groups * band // LANES)
+    return count, -(-groups // count)
+
+
+def by_slot(band, pieces):
+    lane = lax.broadcasted_iota(jnp.int32, pieces[0].shape, 1)
+    out = pieces[-1]
+    for j in range(len(pieces) - 2, -1, -1):
+        out = jnp.where(lane < (j + 1) * band, pieces[j], out)
+    return out
+
+
+def pack(rows, band, start):
+    count, per = packing(band)
+    groups = rows.shape[0] // 8
+    packed = []
+    for v in range(count):
+        pieces = [
+            roll(rows[8 * t : 8 * t + 8], (j - start) * band)
+            for j, t in enumerate(range(v * per, min((v + 1) * per, groups)))
+        ]
+        packed.append(by_slot(band, pieces))
+    return jnp.concatenate(packed, 0)
+
+
+def unpack(blocks, band):
+    _, per = packing(band)
+    out = []
+    for t in range(2 * band // 8):
+        v, j = t // per, t % per
+        out.append(by_slot(band, [roll(b[8 * v : 8 * v + 8], (i - j) * band) for i, b in enumerate(blocks)]))
+    return jnp.concatenate(out, 0)
+
+
 def front_kernel(names, grid, n_k, *refs):
     n_tab = len(names)
     logits_hbm, target_hbm, weight_hbm, kern_hbm = refs[:4]
     tab_hbm = dict(zip(names, refs[4 : 4 + n_tab]))
-    out_ref = refs[4 + n_tab]
-    rest = refs[5 + n_tab :]
-    logits, target, weight, kern = rest[:4]
-    tab = dict(zip(names, rest[4 : 4 + n_tab]))
+    late_hbm = refs[4 + n_tab : 7 + n_tab]
+    out_ref, logits = refs[7 + n_tab : 9 + n_tab]
+    late = refs[9 + n_tab : 12 + n_tab]
+    rest = refs[12 + n_tab :]
+    target, weight, kern = rest[:3]
+    tab = dict(zip(names, rest[3 : 3 + n_tab]))
     (kpad, send1, recv1, zs_own, recv_c, zs_sum, recv2,
-     load_sem, s1, r1, sc, rc, s2, r2) = rest[4 + n_tab :]
+     load_sem, s1, r1, sc, rc, s2, r2) = rest[3 + n_tab :]
 
     tile = logits.shape[0]
     band = kern.shape[-1]
@@ -134,6 +177,12 @@
     for i, name in enumerate(order):
         loads[name] = pltpu.make_async_copy(src[name], dst[name], load_sem.at[i])
         loads[name].start()
+    passed = [
+        pltpu.make_async_copy(a, b, load_sem.at[len(order) + i])
+        for i, (a, b) in enumerate(zip(late_hbm, late))
+    ]
+    for copy in passed:
+        copy.start()
 
     def exists(dr, dc):
         row, col = ty + dr, tx + dc
@@ -171,7 +220,7 @@
     share = mm3(tab["frh"][...], tab["frl"][...], ph, pw)
     for i, (dr, dc) in enumerate(OFFSETS):
         rows = share[(dr + 1) * both : (dr + 2) * both]
-        send1[i] = rows if dc == -1 else pltpu.roll(rows, LANES - (dc + 1) * band, 1)
+        send1[i] = pack(rows, band, dc + 1)
 
     peers = n_c - 1
     for _, (dr, dc) in around:
@@ -201,6 +250,7 @@
     for i, _ in around:
         spec = spec + recv1[i]
 
+    spec = unpack([spec], band)
     sr, si = spec[:band], spec[band:]
     kr, ki = kpad[:, 0], kpad[:, 1]
     ar = (kr * sr - ki * si).reshape(n_k * band, LANES)
@@ -273,8 +323,9 @@
     za = mm3(vh, vl, tab["rbh"][...], tab["rbl"][...])
     za_re = za[:, :LANES].reshape(n_k, band, LANES)
     za_im = za[:, LANES:].reshape(n_k, band, LANES)
-    zs_own[:band] = norm * jnp.sum(kr * za_re + ki * za_im, axis=0)
-    zs_own[band:] = norm * jnp.sum(kr * za_im - ki * za_re, axis=0)
+    zs_re = norm * jnp.sum(kr * za_re + ki * za_im, axis=0)
+    zs_im = norm * jnp.sum(kr * za_im - ki * za_re, axis=0)
+    zs_own[...] = pack(jnp.concatenate([zs_re, zs_im], 0), band, 0)
 
     over = []
     for j in range(1, n_c):
@@ -299,11 +350,8 @@
         def _():
             to_neighbour(zs_sum, recv2, s2, r2, i, dr, dc).wait_recv()
     for er in (-1, 0, 1):
-        acc = jnp.zeros((both, LANES), F32)
-        for ec in (-1, 0, 1):
-            block = recv2[OFFSETS.index((-er, -ec))]
-            acc = acc + (block if ec == -1 else pltpu.roll(block, (ec + 1) * band, 1))
-        out_ref[(er + 1) * both : (er + 2) * both] = acc
+        blocks = [recv2[OFFSETS.index((-er, -ec))] for ec in (-1, 0, 1)]
+        out_ref[(er + 1) * both : (er + 2) * both] = unpack(blocks, band)
 
     for i, (dr, dc) in around:
         @pl.when(exists(dr, dc))
@@ -312,33 +360,42 @@
             to_neighbour(zs_sum, recv2, s2, r2, i, dr, dc).wait_send()
     for copy in over:
         copy.wait_send()
-
-
-def back_kernel(band, z_ref, bch, bcl, brow, logits, new_ref, next_ref, stack):
+    for copy in passed:
+        copy.wait()
+
+
+def back_kernel(band, z_ref, logits, bch, bcl, brow, new_hbm, next_hbm, stack, new, nxt, sem):
     tile = logits.shape[1]
     both = 2 * band
-
-    @pl.when(pl.program_id(0) == 0)
-    def _():
-        zh, zl = split(z_ref[...])
-        wide = mm3(zh, zl, bch[...], bcl[...])
-        rows = []
-        for a in range(3):
-            re = wide[a * both : a * both + band]
-            im = wide[a * both + band : (a + 1) * both]
-            rows += [re[:, :tile] - im[:, tile:], re[:, tile:] + im[:, :tile]]
-        vh, vl = split(jnp.concatenate(rows, 0))
-        n = 3 * both
-        stack[:n] = vh
-        stack[n : 2 * n] = vl
-        stack[2 * n :] = vh
-
-    grad = mm(brow[...], stack[...])
-    x = logits[...]
-    mask = 0.5 * (1.0 + jnp.tanh(x))
-    new = x - STEP_SIZE * grad * (2.0 * mask * (1.0 - mask))
-    new_ref[...] = new
-    next_ref[...] = (0.5 * (1.0 + jnp.tanh(new))).astype(BF)
+    zh, zl = split(z_ref[...])
+    wide = mm3(zh, zl, bch[...], bcl[...])
+    rows = []
+    for a in range(3):
+        re = wide[a * both : a * both + band]
+        im = wide[a * both + band : (a + 1) * both]
+        rows += [re[:, :tile] - im[:, tile:], re[:, tile:] + im[:, :tile]]
+    vh, vl = split(jnp.concatenate(rows, 0))
+    n = 3 * both
+    stack[:n] = vh
+    stack[n : 2 * n] = vl
+    stack[2 * n :] = vh
+
+    chunk = min(tile, 128)
+    copies = []
+    for i in range(tile // chunk):
+        part = slice(i * chunk, (i + 1) * chunk)
+        grad = mm(brow[part], stack[...])
+        x = logits[part]
+        mask = 0.5 * (1.0 + jnp.tanh(x))
+        value = x - STEP_SIZE * grad * (2.0 * mask * (1.0 - mask))
+        new[part] = value
+        nxt[part] = (0.5 * (1.0 + jnp.tanh(value))).astype(BF)
+        for j, (buf, out) in enumerate(((new, new_hbm), (nxt, next_hbm))):
+            copy = pltpu.make_async_copy(buf.at[part], out.at[part], sem.at[2 * i + j])
+            copy.start()
+            copies.append(copy)
+    for copy in copies:
+        copy.wait()
 
 
 def per_device(mask_logits, target_layout, density_weights, socs_kernels):
@@ -351,23 +408,28 @@
     both = 2 * band
     arrays = [mask_logits, target_layout, density_weights, socs_kernels]
     arrays += [jnp.asarray(front[n]) for n in names]
+    late = [jnp.asarray(back[n]) for n in ("bch", "bcl", "brow")]
+    in_vmem = pl.BlockSpec(memory_space=pltpu.VMEM)
+    in_hbm = pl.BlockSpec(memory_space=pl.ANY)
     dma = pltpu.SemaphoreType.DMA
     n_off = len(OFFSETS)
-    zrow = pl.pallas_call(
+    held = 8 * packing(band)[0]
+    kept = pl.pallas_call(
         functools.partial(front_kernel, names, grid, n_k),
-        out_shape=jax.ShapeDtypeStruct((3 * both, LANES), F32),
-        in_specs=[pl.BlockSpec(memory_space=pl.ANY)] * len(arrays),
-        out_specs=pl.BlockSpec(memory_space=pltpu.VMEM),
-        scratch_shapes=[pltpu.VMEM(a.shape, a.dtype) for a in arrays]
+        out_shape=[pltpu.VMEM((3 * both, LANES), F32), pltpu.VMEM((tile, tile), F32)]
+        + [pltpu.VMEM(a.shape, a.dtype) for a in late],
+        in_specs=[in_hbm] * (len(arrays) + len(late)),
+        out_specs=[in_vmem] * (2 + len(late)),
+        scratch_shapes=[pltpu.VMEM(a.shape, a.dtype) for a in arrays[1:]]
         + [
             pltpu.VMEM((n_k, 2, band, LANES), F32),
-            pltpu.VMEM((n_off, both, LANES), F32),
-            pltpu.VMEM((n_off, both, LANES), F32),
-            pltpu.VMEM((both, LANES), F32),
-            pltpu.VMEM((n_c, both, LANES), F32),
-            pltpu.VMEM((both, LANES), F32),
-            pltpu.VMEM((n_off, both, LANES), F32),
-            dma((len(arrays),)),
+            pltpu.VMEM((n_off, held, LANES), F32),
+            pltpu.VMEM((n_off, held, LANES), F32),
+            pltpu.VMEM((held, LANES), F32),
+            pltpu.VMEM((n_c, held, LANES), F32),
+            pltpu.VMEM((held, LANES), F32),
+            pltpu.VMEM((n_off, held, LANES), F32),
+            dma((len(arrays) + len(late),)),
             dma((n_off,)),
             dma((n_off,)),
             dma((n_c,)),
@@ -376,31 +438,26 @@
             dma((n_off,)),
         ],
         compiler_params=pltpu.CompilerParams(
-            collective_id=0, has_side_effects=True, vmem_limit_bytes=60 * 2**20
+            collective_id=0, has_side_effects=True, vmem_limit_bytes=56 * 2**20
         ),
-    )(*arrays)
-
-    blocks = 4
-    rows = tile // blocks
-    whole = lambda shape: pl.BlockSpec(shape, lambda i: (0, 0))
-    by_row = lambda width: pl.BlockSpec((rows, width), lambda i: (i, 0))
+    )(*arrays, *late)
+
     return pl.pallas_call(
         functools.partial(back_kernel, band),
-        grid=(blocks,),
         out_shape=(
             jax.ShapeDtypeStruct((tile, tile), F32),
             jax.ShapeDtypeStruct((tile, tile), BF),
         ),
-        in_specs=[
-            whole((3 * both, LANES)),
-            whole(back["bch"].shape),
-            whole(back["bcl"].shape),
-            by_row(back["brow"].shape[1]),
-            by_row(tile),
+        in_specs=[in_vmem] * 5,
+        out_specs=(in_hbm, in_hbm),
+        scratch_shapes=[
+            pltpu.VMEM((9 * both, tile), BF),
+            pltpu.VMEM((tile, tile), F32),
+            pltpu.VMEM((tile, tile), BF),
+            dma((2 * (tile // min(tile, 128)),)),
         ],
-        out_specs=(by_row(tile), by_row(tile)),
-        scratch_shapes=[pltpu.VMEM((9 * both, tile), BF)],
-    )(zrow, jnp.asarray(back["bch"]), jnp.asarray(back["bcl"]), jnp.asarray(back["brow"]), mask_logits)
+        compiler_params=pltpu.CompilerParams(vmem_limit_bytes=16 * 2**20),
+    )(*kept)
 
 
 def solution(mesh):

time: 25.7 us -> 21.6 us (0.84)
  Pallas kernels: 24.8 us -> 20.9 us
    pallas_call x1, Pallas kernels: 4.66 us -> 1.84 us  [per_device(): pl.pallas_call(functools.partial(back_kernel, band), out_shape=(jax.Shape...]
    pallas_call x1, Pallas kernels: 20.2 us -> 19 us  [per_device(): pl.pallas_call(functools.partial(front_kernel, names, grid, n_k), out_sha...]
where the time goes in v2:
time: 21.6 us; the launch traced here: 21.5 us
  Pallas kernels  20.9 us (97%)
  between operations  0.64 us (3%)
    pallas_call x1, Pallas kernels, per_device(): pl.pallas_call(functools.partial(front_kernel, names, grid, n_k), out_sha...  19 us
    pallas_call x1, Pallas kernels, per_device(): pl.pallas_call(functools.partial(back_kernel, band), out_shape=(jax.Shape...  1.84 us

profile of v2, /device:TPU:1, one launch (start us, length us, event | category | flops | bytes accessed | tf_op | source)
XLA Modules:
  0.0 21.5 jit_solution(6339058577776256198)
XLA Ops:
  0.6 19.0 %shard_map.230 = (f32[144,128]{1,0:T(8,128)S(1)}, f32[512,512]{1,0:T(8,128)S(1)}, bf16[128,1024]{1,0:T(8,128)(2,1)S(1)}, bf16[128,1024]{1,0:T(8,128)(2,1)S(1)}, bf16[512,432]{1,0:T(8,128)(2,1)S(1)}) custom-call(f32[512,512]{1,0:T(8,128)} %refs_0_.1, s32[512,512]{1,0:T(8,128)} %refs_1_.1, s32[512,512]{1,0:T(8,128)} %refs_2_.1, f32[1,12,2,24,24]{4,3,2,1,0:T(8,128)} %refs_3_.1, ...), custom_call_target="tpu_custom_call" | custom-call | tf_op jit(solution)/shard_map/pallas_call | solution.py:417
  19.7 1.8 %shard_map.231 = (f32[512,512]{1,0:T(8,128)}, bf16[512,512]{1,0:T(8,128)(2,1)}) custom-call(f32[144,128]{1,0:T(8,128)S(1)} %get-tuple-element.7.z_ref, f32[512,512]{1,0:T(8,128)S(1)} %get-tuple-element.8.logits, bf16[128,1024]{1,0:T(8,128)(2,1)S(1)} %get-tuple-element.9.bch, bf16[128,1024]{1,0:T(8,128)(2,1)S(1)} %get-tuple-element.10.bcl, ...), custom_call_target="tpu_custom_call" | custom-call | tf_op jit(solution)/shard_map/pallas_call | solution.py:445
